TPU v7x, 256 devices: a whole 4x4x8 slice. The times are simulated.
256 devices in a mesh: blk: 128 (over x_hi, z, y, core), grp: 2 (over x_lo).
Axes of the slice: x: 4 (x_hi: 2, x_lo: 2; x = x_hi * 2 + x_lo), y: 4, z: 8, core: 2. Of those that a mesh axis runs over, the one named last changes fastest.
Arguments:
- layer_one: bfloat16 [14336, 1024], P(('blk', 'grp')), may hold values from -6 to 6
- layer_two: bfloat16 [14336, 1024], P(('blk', 'grp')), may hold values from -6 to 6
- spread: int32 [2], replicated, may hold values from 1024 to 4096
Outputs:
- profiles: float32 [2, 14336], P(None, ('blk', 'grp'))
- alignment: float32 [], replicated
All inputs are finite; a program needn't handle non-finite values.
Results may differ from a plain program's by a relative error of at most 0.0003.
Values may be sent and summed in bfloat16 or wider, within the bound.
No kernel may reach another device: no remote copies, remote signals or barrier semaphores. Data moves between devices by JAX's collectives and lax.ppermute only.
A program may use at most 128 MiB of HBM per device.

v0:
```python
import functools
import jax
import jax.numpy as jnp
from jax import lax
from jax.sharding import Mesh
from jax.sharding import PartitionSpec as P

D = 1024
BLK = ("blk_0", "blk_1", "blk_2", "blk_3")
BLK_GRP = ("blk_0", "blk_1", "blk_2", "blk_3", "grp")


def by_axis(array, axes):
    return functools.reduce(lax.psum, axes, array)


def kernel_block(rows, sq_rows, cols, scale, offset):
    sq_cols = jnp.sum(cols.astype(jnp.float32) ** 2, axis=1)
    inner = lax.dot_general(
        rows, cols, (((1,), (1,)), ((), ())), preferred_element_type=jnp.float32
    )
    dist = sq_rows[:, None] + sq_cols[None, :] - 2.0 * inner
    return jnp.exp(-dist / (2.0 * scale)) - offset


def shards(layer_one, layer_two, spread):
    scales = spread.astype(jnp.float32)
    offsets = jnp.exp(-D / scales)
    stacked = jnp.stack([layer_one, layer_two])
    paired = lax.all_gather(stacked, "grp", axis=1, tiled=True)
    sq_pair = jnp.sum(paired.astype(jnp.float32) ** 2, axis=2)
    block = lax.all_gather(stacked, BLK, axis=1, tiled=True)
    first = kernel_block(paired[0], sq_pair[0], block[0], scales[0], offsets[0])
    second = kernel_block(paired[1], sq_pair[1], block[1], scales[1], offsets[1])
    first, second = (first, second)
    rows_acc = jnp.stack([jnp.sum(first, axis=1), jnp.sum(second, axis=1)])
    prods = jnp.stack([jnp.sum(first * second), jnp.sum(first * first), jnp.sum(second * second)])
    rows_acc, prods = (rows_acc, prods)
    own_rows = lax.psum_scatter(rows_acc, "grp", scatter_dimension=1, tiled=True)
    total = own_rows.shape[1] * lax.axis_size(BLK) * lax.axis_size("grp")
    row_terms = jnp.stack(
        [
            jnp.sum(own_rows[0]),
            jnp.sum(own_rows[1]),
            jnp.sum(own_rows[0] * own_rows[1]),
            jnp.sum(own_rows[0] * own_rows[0]),
            jnp.sum(own_rows[1] * own_rows[1]),
        ]
    )
    prods = by_axis(prods, BLK_GRP)
    row_terms = by_axis(row_terms, BLK_GRP)
    sum_one, sum_two = (row_terms[0], row_terms[1])
    c_cross, c_one, c_two = (row_terms[2], row_terms[3], row_terms[4])
    h_cross = prods[0] - 2.0 * c_cross / total + sum_one * sum_two / (total * total)
    h_one = prods[1] - 2.0 * c_one / total + sum_one * sum_one / (total * total)
    h_two = prods[2] - 2.0 * c_two / total + sum_two * sum_two / (total * total)
    alignment = h_cross / jnp.sqrt(h_one * h_two)
    profiles = jnp.stack(
        [own_rows[0] / jnp.sqrt(c_one / total), own_rows[1] / jnp.sqrt(c_two / total)]
    )
    return (profiles, alignment)


def solution(mesh):
    finer = Mesh(
        mesh.devices.reshape(2, 8, 4, 2, mesh.shape["grp"]),
        ("blk_0", "blk_1", "blk_2", "blk_3", "grp"),
    )
    return jax.shard_map(
        shards,
        mesh=finer,
        in_specs=(P(BLK_GRP, None), P(BLK_GRP, None), P()),
        out_specs=(P(None, BLK_GRP), P()),
        check_vma=False,
    )
```

profile of v0, /device:TPU:1, one launch (start us, length us, event | category | flops | bytes accessed | tf_op | source)
XLA Modules:
  0.0 312.2 jit_solution(16533642095395601667)
XLA Ops:
  7.2 0.0 all-gather.2.cloned.1.call-start
  7.2 1.7 pad_maximum_fusion
  8.9 0.0 all-gather.2.cloned.1.call-update
  8.9 0.7 convert_element_type.14
  9.6 0.6 fusion.16
  11.5 1.3 dynamic-slice
  13.4 0.7 divide_exponential_fusion
  14.0 0.6 fusion.17
  14.6 6.9 %all_gather.6 = bf16[2,112,1024]{2,1,0:T(8,128)(2,1)S(1)} all-gather(bf16[2,56,1024]{2,1,0:T(8,128)(2,1)} %pad_maximum_fusion), channel_id=1, replica_groups=mesh['blk_0'=2,'blk_1'=8,'blk_2'=4,'blk_3'=2,'grp'=2] {'grp'}, dimensions={1}, use_global_device_ids=true | all-gather | bytes 688128 | tf_op jit(solution)/shard_map/all_gather | solution.py:30
  21.5 0.2 multiply_reduce_fusion.5
  21.7 191.0 %all-gather.2.cloned.1.call-done = bf16[2,7168,1024]{2,1,0:T(8,128)(2,1)} async-done(((bf16[2,56,1024]{2,1,0:T(8,128)(2,1)}), bf16[2,7168,1024]{2,1,0:T(8,128)(2,1)}) %all-gather.2.cloned.1.call-update) | async-done | bytes 29360144 | tf_op jit(solution)/shard_map/all_gather | solution.py:32
  212.6 12.8 %multiply_reduce_fusion.1 = (f32[7168]{0:T(1024)S(1)}, f32[7168]{0:T(1024)S(1)}) fusion(bf16[2,7168,1024]{2,1,0:T(8,128)(2,1)} %all-gather.2.cloned.1.call-done), kind=kLoop, calls=%fused_computation.1 | loop fusion | flops 44025856 | bytes 29417472 | tf_op jit(solution)/shard_map/reduce_sum | solution.py:18
  225.4 9.0 %fusion.10 = f32[112,7168]{1,0:T(8,128)S(1)} fusion(bf16[2,7168,1024]{2,1,0:T(8,128)(2,1)} %all-gather.2.cloned.1.call-done, f32[]{:T(128)} %bitcast.12, f32[]{:T(128)} %bitcast.11, f32[7168]{0:T(1024)S(1)} %get-tuple-element.3, f32[112]{0:T(128)S(1)} %get-tuple-element.26, bf16[2,112,1024]{2,1,0:T(8,128)(2,1)S(1)} %all_gather.6), kind=kOutput, calls=%fused_computation.14 | convolution fusion | flops 1648984064 | bytes 18150912 | tf_op jit(solution)/shard_map/dot_general | solution.py:19
  234.5 10.3 %multiply_reduce_fusion.4 = (f32[]{:T(128)}, f32[]{:T(128)}, f32[112]{0:T(128)S(1)}, f32[]{:T(128)}, f32[112]{0:T(128)S(1)}) fusion(f32[112,7168]{1,0:T(8,128)S(1)} %fusion.10, f32[]{:T(128)} %bitcast.6, f32[]{:T(128)} %bitcast.5, bf16[2,7168,1024]{2,1,0:T(8,128)(2,1)} %all-gather.2.cloned.1.call-done, bf16[2,112,1024]{2,1,0:T(8,128)(2,1)S(1)} %all_gather.6, ...), kind=kOutput, calls=%fused_computation.20 | convolution fusion | flops 1655406336 | bytes 18151820 | tf_op jit(solution)/shard_map/dot_general | solution.py:19
  244.8 3.8 %all-reduce = f32[2,112]{1,0:T(2,128)S(1)} all-reduce(f32[2,112]{1,0:T(2,128)S(1)} %pad_maximum_fusion.1), channel_id=2, replica_groups=mesh['blk_0'=2,'blk_1'=8,'blk_2'=4,'blk_3'=2,'grp'=2] {'grp'}, use_global_device_ids=true, to_apply=%region_5.0.clone | all-reduce | flops 224 | bytes 1792
  248.5 0.1 constant_dynamic-slice_fusion
  248.6 0.7 multiply_reduce_fusion.6
  249.3 2.0 pad_maximum_fusion.3
  251.3 3.2 %stack.64 = f32[5]{0:T(128)S(1)} concatenate(f32[1]{0:T(128)} %bitcast.14, f32[1]{0:T(128)} %bitcast.15, f32[1]{0:T(128)} %bitcast.16, f32[1]{0:T(128)} %bitcast.17, f32[1]{0:T(128)} %bitcast.18), dimensions={0} | concatenate | bytes 40 | tf_op jit(solution)/shard_map/stack | solution.py:41
  254.5 5.3 %all-reduce.5 = (f32[5]{0:T(128)S(1)}, f32[3]{0:T(128)S(1)}) all-reduce(f32[5]{0:T(128)S(1)} %stack.64, f32[3]{0:T(128)S(1)} %pad_maximum_fusion.3), channel_id=1, replica_groups=mesh['blk_0'=2,'blk_1'=8,'blk_2'=4,'blk_3'=2,'grp'=2] {'blk_0'}, use_global_device_ids=true, to_apply=%region_11.0 | all-reduce | flops 8 | bytes 64 | tf_op jit(solution)/shard_map/psum | solution.py:14
  259.8 11.7 %all-reduce.1 = (f32[5]{0:T(128)S(1)}, f32[3]{0:T(128)S(1)}) all-reduce(f32[5]{0:T(128)S(1)} %get-tuple-element.22, f32[3]{0:T(128)S(1)} %get-tuple-element.23), channel_id=1, replica_groups=mesh['blk_0'=2,'blk_1'=8,'blk_2'=4,'blk_3'=2,'grp'=2] {'blk_1'}, use_global_device_ids=true, to_apply=%region_12.0 | all-reduce | flops 8 | bytes 64 | tf_op jit(solution)/shard_map/psum | solution.py:14
  271.5 8.4 %all-reduce.2 = (f32[5]{0:T(128)S(1)}, f32[3]{0:T(128)S(1)}) all-reduce(f32[5]{0:T(128)S(1)} %get-tuple-element.14, f32[3]{0:T(128)S(1)} %get-tuple-element.15), channel_id=1, replica_groups=mesh['blk_0'=2,'blk_1'=8,'blk_2'=4,'blk_3'=2,'grp'=2] {'blk_2'}, use_global_device_ids=true, to_apply=%region_13.0 | all-reduce | flops 8 | bytes 64 | tf_op jit(solution)/shard_map/psum | solution.py:14
  280.0 10.4 %all-reduce.4 = (f32[5]{0:T(128)S(1)}, f32[3]{0:T(128)S(1)}) all-reduce(f32[5]{0:T(128)S(1)} %get-tuple-element.16, f32[3]{0:T(128)S(1)} %get-tuple-element.17), channel_id=1, replica_groups=mesh['blk_0'=2,'blk_1'=8,'blk_2'=4,'blk_3'=2,'grp'=2] {'blk_3'}, use_global_device_ids=true, to_apply=%region_14.0 | all-reduce | flops 8 | bytes 64 | tf_op jit(solution)/shard_map/psum | solution.py:14
  290.4 3.8 %all-reduce.3 = (f32[5]{0:T(128)S(1)}, f32[3]{0:T(128)S(1)}) all-reduce(f32[5]{0:T(128)S(1)} %get-tuple-element.20, f32[3]{0:T(128)S(1)} %get-tuple-element.21), channel_id=1, replica_groups=mesh['blk_0'=2,'blk_1'=8,'blk_2'=4,'blk_3'=2,'grp'=2] {'grp'}, use_global_device_ids=true, to_apply=%region_15.0 | all-reduce | flops 8 | bytes 64 | tf_op jit(solution)/shard_map/psum | solution.py:14
  294.2 0.7 fusion.14
  303.7 0.6 pad_maximum_fusion.2
  (3 shorter events, 0.0 us)
Async XLA Ops:
  7.2 205.5 %all-gather.2.cloned.1.call-start = ((), (), s32[]{:S(2)}) async-start(), calls=%async_computation | async-start | bytes 29589504 | tf_op jit(solution)/shard_map/all_gather | solution.py:32
Sparse Core Ops, SparseCore 0:
  11.7 200.9 all-gather.1
where the time goes:
time: 313 us; the launch traced here: 312 us
  waiting for transfers between devices  191 us (61%)
  blocking collectives  50.3 us (16%)
  between operations  26 us (8%)
  matrix products  19.3 us (6%)
  other arithmetic  19.2 us (6%)
  local copies, waits for them, and re-layouts  6.45 us (2%)
    all_gather x1, waiting for transfers between devices, shards(): block = lax.all_gather(stacked, BLK, axis=1, tiled=True)  191 us
    psum x5, blocking collectives, by_axis(): return functools.reduce(lax.psum, axes, array)  39.7 us
    dot_general x2, matrix products, kernel_block(): lax.dot_general(rows, cols, (((1,), (1,)), ((), ())), preferred_element_t...  19.3 us
    reduce_sum x1, other arithmetic, kernel_block(): sq_cols = jnp.sum(cols.astype(jnp.float32) ** 2, axis=1)  12.8 us
    all_gather x1, blocking collectives, shards(): paired = lax.all_gather(stacked, 'grp', axis=1, tiled=True)  6.85 us
  transfers between devices with their start and end apart: 1, of which 1 were waited for; matrix products, arithmetic and copies ran while one was open for 1% of the time, Pallas kernels for 0%

commit v1 on v0

--- a/solution.py
+++ b/solution.py
@@ -4,10 +4,20 @@
 from jax import lax
 from jax.sharding import Mesh
 from jax.sharding import PartitionSpec as P
+from jax.lax import all_to_all, axis_size
 
 D = 1024
 BLK = ("blk_0", "blk_1", "blk_2", "blk_3")
 BLK_GRP = ("blk_0", "blk_1", "blk_2", "blk_3", "grp")
+
+
+def feed_cells_up(target, d0, mesh_name):
+    return jnp.concatenate(
+        all_to_all(jnp.stack(axis_size(mesh_name) * [target]), mesh_name, 0, 0), axis=d0
+    )
+
+
+unite_the_stocks = functools.partial(feed_cells_up, d0=1, mesh_name=BLK)
 
 
 def by_axis(array, axes):
@@ -29,7 +39,7 @@
     stacked = jnp.stack([layer_one, layer_two])
     paired = lax.all_gather(stacked, "grp", axis=1, tiled=True)
     sq_pair = jnp.sum(paired.astype(jnp.float32) ** 2, axis=2)
-    block = lax.all_gather(stacked, BLK, axis=1, tiled=True)
+    block = unite_the_stocks(stacked)
     first = kernel_block(paired[0], sq_pair[0], block[0], scales[0], offsets[0])
     second = kernel_block(paired[1], sq_pair[1], block[1], scales[1], offsets[1])
     first, second = (first, second)

time: 313 us -> 815 us (2.60)
  waiting for transfers between devices: 191 us -> 568 us
  blocking collectives: 50.3 us -> 135 us
  local copies, waits for them, and re-layouts: 6.45 us -> 38.1 us
  starting transfers between devices: 0.04 us -> 16.9 us
  between operations: 26 us -> 12.7 us
    all_to_all x0 -> x1, waiting for transfers between devices: none -> 568 us  [feed_cells_up(): all_to_all(jnp.stack(axis_size(mesh_name) * [target]), mesh_name, 0, 0)]
    all_gather x1 -> x0, waiting for transfers between devices: 191 us -> none  [shards(): block = lax.all_gather(stacked, BLK, axis=1, tiled=True)]
    all_gather x1, blocking collectives: 6.85 us -> 70.9 us  [shards(): paired = lax.all_gather(stacked, 'grp', axis=1, tiled=True)]
    slice x0 -> x1, local copies, waits for them, and re-layouts: none -> 22.1 us  [shards(): block[1]]
    all_to_all x0 -> x1, starting transfers between devices: none -> 16.9 us  [feed_cells_up(): all_to_all(jnp.stack(axis_size(mesh_name) * [target]), mesh_name, 0, 0)]
    unnamed x1, blocking collectives: 3.77 us -> 15.6 us
    another operation x0 -> x1, local copies, waits for them, and re-layouts: none -> 10.1 us  [feed_cells_up(): jnp.stack(axis_size(mesh_name) * [target])]
    psum x5, blocking collectives: 39.7 us -> 48.3 us  [by_axis(): return functools.reduce(lax.psum, axes, array)]
  transfers between devices with their start and end apart: 1 -> 1, of which waited for: 1 -> 1; matrix products, arithmetic and copies ran while one was open for 1% -> 0% of each run, Pallas kernels for 0% -> 0%
where the time goes in v1:
time: 815 us; the launch traced here: 814 us
  waiting for transfers between devices  568 us (70%)
  blocking collectives  135 us (17%)
  local copies, waits for them, and re-layouts  38.1 us (5%)
  matrix products  25.6 us (3%)
  other arithmetic  17.5 us (2%)
  starting transfers between devices  16.9 us (2%)
  between operations  12.7 us (2%)
    all_to_all x1, waiting for transfers between devices, feed_cells_up(): all_to_all(jnp.stack(axis_size(mesh_name) * [target]), mesh_name, 0, 0)  568 us
    all_gather x1, blocking collectives, shards(): paired = lax.all_gather(stacked, 'grp', axis=1, tiled=True)  70.9 us
    psum x5, blocking collectives, by_axis(): return functools.reduce(lax.psum, axes, array)  48.3 us
    dot_general x2, matrix products, kernel_block(): lax.dot_general(rows, cols, (((1,), (1,)), ((), ())), preferred_element_t...  25.6 us
    slice x1, local copies, waits for them, and re-layouts, shards(): block[1]  22.1 us
    all_to_all x1, starting transfers between devices, feed_cells_up(): all_to_all(jnp.stack(axis_size(mesh_name) * [target]), mesh_name, 0, 0)  16.9 us
  transfers between devices with their start and end apart: 1, of which 1 were waited for; matrix products, arithmetic and copies ran while one was open for 0% of the time, Pallas kernels for 0%

profile of v1, /device:TPU:1, one launch (start us, length us, event | category | flops | bytes accessed | tf_op | source)
XLA Modules:
  0.0 813.6 jit_solution(7591221915463627001)
XLA Ops:
  0.6 1.0 pad_maximum_fusion
  1.6 10.1 %stack.39 = bf16[128,2,56,1024]{3,2,1,0:T(8,128)(2,1)} broadcast(bf16[2,56,1024]{2,1,0:T(8,128)(2,1)S(1)} %pad_maximum_fusion), dimensions={1,2,3} | broadcast | bytes 29589504 | tf_op jit(solution)/shard_map/stack | solution.py:16
  11.7 0.0 copy-start
  11.7 0.0 copy-start.1
  11.7 16.9 %all-to-all-start = ((bf16[128,2,56,1024]{3,2,1,0:T(8,128)(2,1)}), bf16[128,2,56,1024]{3,2,1,0:T(8,128)(2,1)}, u32[]{:S(2)}, u32[]{:S(2)}) async-start(bf16[128,2,56,1024]{3,2,1,0:T(8,128)(2,1)} %stack.39), calls=%async_computation | async-start | bytes 58720256 | tf_op jit(solution)/shard_map/all_to_all | solution.py:16
  28.6 0.0 copy-done
  28.7 0.6 fusion.13
  30.5 0.0 copy-done.1
  30.6 0.6 dynamic-slice
  31.8 0.6 fusion.14
  32.4 70.9 %all_gather.3 = bf16[2,112,1024]{2,1,0:T(8,128)(2,1)S(1)} all-gather(bf16[2,56,1024]{2,1,0:T(8,128)(2,1)S(1)} %pad_maximum_fusion), channel_id=1, replica_groups=mesh['blk_0'=2,'blk_1'=8,'blk_2'=4,'blk_3'=2,'grp'=2] {'grp'}, dimensions={1}, use_global_device_ids=true | all-gather | bytes 688128 | tf_op jit(solution)/shard_map/all_gather | solution.py:40
  103.3 0.2 multiply_reduce_fusion.5
  103.5 567.9 %all-to-all-done = bf16[128,2,56,1024]{3,2,1,0:T(8,128)(2,1)} async-done(((bf16[128,2,56,1024]{3,2,1,0:T(8,128)(2,1)}), bf16[128,2,56,1024]{3,2,1,0:T(8,128)(2,1)}, u32[]{:S(2)}, u32[]{:S(2)}) %all-to-all-start) | async-done | bytes 29360160 | tf_op jit(solution)/shard_map/all_to_all | solution.py:16
  671.4 22.1 %fusion.10 = (bf16[1,128,56,1024]{3,2,0,1:T(8,128)(2,1)}, bf16[1,128,56,1024]{3,2,0,1:T(8,128)(2,1)}) fusion(bf16[2,128,56,1024]{3,2,0,1:T(8,128)(2,1)} %bitcast.3), kind=kLoop, calls=%fused_computation.35 | loop fusion | bytes 58720256 | tf_op jit(solution)/shard_map/slice | solution.py:44
  693.5 13.1 %multiply_reduce_fusion.1 = (f32[128,56]{1,0:T(8,128)S(1)}, f32[128,56]{1,0:T(8,128)S(1)}) fusion(bf16[2,128,56,1024]{3,2,0,1:T(8,128)(2,1)} %bitcast.3), kind=kLoop, calls=%fused_computation.1 | loop fusion | flops 44025856 | bytes 29417472 | tf_op jit(solution)/shard_map/reduce_sum | solution.py:28
  706.6 0.1 add.77
  706.7 0.1 add.72
  706.8 12.5 %fusion.6 = f32[112,7168]{1,0:T(8,128)} fusion(bf16[7168,1024]{1,0:T(8,128)(2,1)} %bitcast.40, f32[]{:T(128)} %bitcast.13, f32[]{:T(128)} %bitcast.12, f32[7168]{0:T(1024)S(1)} %add.77, f32[112]{0:T(128)S(1)} %get-tuple-element.28, bf16[2,112,1024]{2,1,0:T(8,128)(2,1)S(1)} %all_gather.3), kind=kOutput, calls=%fused_computation.10 | convolution fusion | flops 1648984064 | bytes 18149896 | tf_op jit(solution)/shard_map/dot_general | solution.py:29
  719.3 13.1 %multiply_reduce_fusion.4 = (f32[]{:T(128)}, f32[]{:T(128)}, f32[112]{0:T(128)S(1)}, f32[]{:T(128)}, f32[112]{0:T(128)S(1)}) fusion(f32[112,7168]{1,0:T(8,128)} %fusion.6, f32[]{:T(128)} %bitcast.7, f32[]{:T(128)} %bitcast.6, bf16[7168,1024]{1,0:T(8,128)(2,1)} %bitcast.39, bf16[2,112,1024]{2,1,0:T(8,128)(2,1)S(1)} %all_gather.3, f32[7168]{0:T(1024)S(1)} %add.72, ...), kind=kOutput, calls=%fused_computation.16 | convolution fusion | flops 1655406336 | bytes 18150804 | tf_op jit(solution)/shard_map/dot_general | solution.py:29
  732.4 15.6 %all-reduce = f32[2,112]{1,0:T(2,128)S(1)} all-reduce(f32[2,112]{1,0:T(2,128)S(1)} %pad_maximum_fusion.1), channel_id=2, replica_groups=mesh['blk_0'=2,'blk_1'=8,'blk_2'=4,'blk_3'=2,'grp'=2] {'grp'}, use_global_device_ids=true, to_apply=%region_5.0.clone | all-reduce | flops 224 | bytes 1792
  748.0 0.1 constant_dynamic-slice_fusion
  748.0 0.7 multiply_reduce_fusion.6
  748.7 2.0 pad_maximum_fusion.3
  750.7 3.2 stack.48
  754.0 5.3 all-reduce.5
  759.2 22.5 %all-reduce.1 = (f32[5]{0:T(128)S(1)}, f32[3]{0:T(128)S(1)}) all-reduce(f32[5]{0:T(128)S(1)} %get-tuple-element.22, f32[3]{0:T(128)S(1)} %get-tuple-element.23), channel_id=1, replica_groups=mesh['blk_0'=2,'blk_1'=8,'blk_2'=4,'blk_3'=2,'grp'=2] {'blk_1'}, use_global_device_ids=true, to_apply=%region_12.0 | all-reduce | flops 8 | bytes 64 | tf_op jit(solution)/shard_map/psum | solution.py:24
  781.7 6.1 all-reduce.2
  787.9 10.7 %all-reduce.4 = (f32[5]{0:T(128)S(1)}, f32[3]{0:T(128)S(1)}) all-reduce(f32[5]{0:T(128)S(1)} %get-tuple-element.16, f32[3]{0:T(128)S(1)} %get-tuple-element.17), channel_id=1, replica_groups=mesh['blk_0'=2,'blk_1'=8,'blk_2'=4,'blk_3'=2,'grp'=2] {'blk_3'}, use_global_device_ids=true, to_apply=%region_14.0 | all-reduce | flops 8 | bytes 64 | tf_op jit(solution)/shard_map/psum | solution.py:24
  798.5 3.8 all-reduce.3
  802.3 0.7 fusion.11
  811.2 0.6 pad_maximum_fusion.2
  (5 shorter events, 0.0 us)
Async XLA Ops:
  11.7 17.0 %copy-start = (s32[2]{0:T(128)S(1)}, s32[2]{0:T(128)}, u32[]{:S(2)}) copy-start(s32[2]{0:T(128)} %param.5) | copy-start | bytes 28
  11.7 18.9 %copy-start.1 = (u32[256]{0:T(256)S(1)}, u32[256]{0:T(256)}, u32[]{:S(2)}) copy-start(u32[256]{0:T(256)} %constant.38) | copy-start | bytes 3076
  11.7 659.7 %all-to-all-start = ((bf16[128,2,56,1024]{3,2,1,0:T(8,128)(2,1)}), bf16[128,2,56,1024]{3,2,1,0:T(8,128)(2,1)}, u32[]{:S(2)}, u32[]{:S(2)}) async-start(bf16[128,2,56,1024]{3,2,1,0:T(8,128)(2,1)} %stack.39), calls=%async_computation | async-start | bytes 58720256 | tf_op jit(solution)/shard_map/all_to_all | solution.py:16
